TPU v7x, 32 devices: a whole 2x2x4 slice. The times are simulated.
32 devices in a mesh: prow: 4 (over y, core), pcol: 8 (over z, x).
Axes of the slice: x: 2, y: 2, z: 4, core: 2. Of those that a mesh axis runs over, the one named last changes fastest.
Arguments:
- matrix: bfloat16 [14336, 4096], P('prow', 'pcol'), may hold values from -6 to 6
- u_inverse: float32 [2, 512, 512], replicated, may hold values from -0.02 to 0.2, as said below
- l_inverse: float32 [2, 512, 512], replicated, may hold values from -0.02 to 0.2, as said below
Outputs:
- factored: bfloat16 [14336, 4096], P('prow', 'pcol')
Inputs may be any that keep to these rules, and one draw needn't show every extreme that they name: u_inverse[p] is upper triangular with positive diagonal. l_inverse[p] is lower triangular with positive diagonal.
All inputs are finite; a program needn't handle non-finite values.
Results may differ from a plain program's by a relative error of at most 0.008.
Values may be sent and summed in bfloat16 or wider, within the bound.
A program may use at most 64 MiB of HBM per device.

v0:
```python
import jax
import jax.numpy as jnp
from jax import lax
from jax.sharding import PartitionSpec as P


def broadcast(block, axis, holder):
    block = jnp.where(lax.axis_index(axis) == holder, block, jnp.zeros_like(block))
    return lax.psum(block, axis)


def body(matrix, u_inverse, l_inverse):
    width = matrix.shape[1]
    prow_index = lax.axis_index("prow")
    pcol_index = lax.axis_index("pcol")
    row_ids = jnp.arange(matrix.shape[0]) // width * lax.axis_size("prow") + prow_index

    def lower_factor(current, panel_id):
        panel = current.astype(jnp.float32)
        lower = jnp.dot(panel, u_inverse[panel_id], precision=lax.Precision.HIGHEST).astype(
            jnp.bfloat16
        )
        lower = broadcast(lower, "pcol", panel_id)
        return jnp.where(row_ids[:, None] > panel_id, lower, jnp.zeros_like(lower))

    def upper_factor(head, panel_id):
        upper = jnp.dot(
            l_inverse[panel_id], head.astype(jnp.float32), precision=lax.Precision.HIGHEST
        ).astype(jnp.bfloat16)
        upper = broadcast(upper, "prow", panel_id)
        return jnp.where(pcol_index > panel_id, upper, jnp.zeros_like(upper))

    def apply_update(block, lower, upper, block_ids, panel_id):
        product = jnp.dot(lower, upper, preferred_element_type=jnp.float32)
        fresh = (block.astype(jnp.float32) - product).astype(jnp.bfloat16)
        keep_lower = (block_ids[:, None] > panel_id) & (pcol_index == panel_id)
        return jnp.where(keep_lower, lower, fresh)

    def place_upper(head, upper, panel_id):
        return jnp.where((prow_index == panel_id) & (pcol_index > panel_id), upper, head)

    lower = lower_factor(matrix, 0)
    upper = upper_factor(matrix[:width], 0)
    head = apply_update(matrix[:width], lower[:width], upper, row_ids[:width], 0)
    head = place_upper(head, upper, 0)
    upper_next = upper_factor(head, 1)
    tail = apply_update(matrix[width:], lower[width:], upper, row_ids[width:], 0)
    current = jnp.concatenate([head, tail], 0)
    lower_next = lower_factor(current, 1)
    current = apply_update(current, lower_next, upper_next, row_ids, 1)
    current = current.at[:width].set(place_upper(current[:width], upper_next, 1))
    return current


def solution(mesh):
    in_specs = (P("prow", "pcol"), P(), P())
    out_specs = P("prow", "pcol")
    return jax.shard_map(body, mesh=mesh, in_specs=in_specs, out_specs=out_specs, check_vma=False)
```

profile of v0, /device:TPU:28, one launch (start us, length us, event | category | flops | bytes accessed | tf_op | source)
XLA Modules:
  0.0 394.3 jit_solution(16008264006359029436)
XLA Ops:
  6.5 9.2 %fusion.1 = bf16[3584,512]{1,0:T(8,128)(2,1)} fusion(bf16[3584,512]{1,0:T(8,128)(2,1)} %param.5, pred[]{:T(512)S(6)} %eq.19, f32[2,512,512]{2,1,0:T(8,128)} %param.6), kind=kOutput, calls=%fused_computation.5 | convolution fusion | flops 11277959168 | bytes 8388609 | tf_op jit(solution)/shard_map/dot_general | solution.py:20
  15.7 0.0 all-reduce.7.cloned.1.call-update
  15.8 0.0 all-reduce.5.cloned.1.call-start
  15.8 1.5 copy-done
  17.3 2.8 fusion.11
  20.2 0.0 all-reduce.5.cloned.1.call-update
  20.2 0.0 all-reduce.11.cloned.1.call-start
  20.3 137.3 %all-reduce.7.cloned.1.call-done = bf16[3584,512]{1,0:T(8,128)(2,1)} async-done(((bf16[3584,512]{1,0:T(8,128)(2,1)}), bf16[3584,512]{1,0:T(8,128)(2,1)}) %all-reduce.7.cloned.1.call-update) | async-done | bytes 3670032 | tf_op jit(solution)/shard_map/psum | solution.py:9
  157.6 4.5 %broadcast_select_fusion = bf16[3584,512]{1,0:T(8,128)(2,1)} fusion(bf16[3584,512]{1,0:T(8,128)(2,1)} %all-reduce.7.cloned.1.call-done, pred[3584]{0:T(1024)(128)(4,1)S(1)} %broadcast_compare_fusion), kind=kLoop, calls=%fused_computation.10 | loop fusion | flops 1835008 | bytes 7343616 | tf_op jit(solution)/shard_map/jit(_where)/select_n | solution.py:24
  162.1 31.4 %all-reduce.5.cloned.1.call-done = bf16[512,512]{1,0:T(8,128)(2,1)} async-done(((bf16[512,512]{1,0:T(8,128)(2,1)}), bf16[512,512]{1,0:T(8,128)(2,1)}) %all-reduce.5.cloned.1.call-update) | async-done | bytes 524304 | tf_op jit(solution)/shard_map/psum | solution.py:9
  193.5 2.2 fusion.10
  195.7 2.0 fusion.13
  197.7 0.0 all-reduce.11.cloned.1.call-update
  197.7 0.0 copy-start.1
  197.8 0.2 all-reduce.9.cloned.1.call-start
  198.0 5.7 %fusion.3 = bf16[3072,512]{1,0:T(8,128)(2,1)S(1)} fusion(bf16[3584,512]{1,0:T(8,128)(2,1)} %broadcast_select_fusion, bf16[3584,512]{1,0:T(8,128)(2,1)} %param.5, pred[3072]{0:T(1024)(128)(4,1)S(1)} %fusion.33, bf16[512,512]{1,0:T(8,128)(2,1)S(1)} %copy-done.2, pred[]{:T(512)S(6)} %gt.44), kind=kOutput, calls=%fused_computation.7 | convolution fusion | flops 1617166336 | bytes 13110273 | tf_op jit(solution)/shard_map/dot_general | solution.py:34
  203.7 1.7 copy-done.3
  205.4 8.1 %fusion.2 = bf16[3584,512]{1,0:T(8,128)(2,1)} fusion(pred[]{:T(512)S(6)} %eq.8, bf16[3072,512]{1,0:T(8,128)(2,1)S(1)} %fusion.3, bf16[512,512]{1,0:T(8,128)(2,1)S(1)} %fusion.10, f32[2,512,512]{2,1,0:T(8,128)S(1)} %copy-done.1), kind=kOutput, calls=%fused_computation.6 | convolution fusion | flops 11285299200 | bytes 8388609 | tf_op jit(solution)/shard_map/dot_general | solution.py:20
  213.5 0.0 all-reduce.9.cloned.1.call-update
  213.5 17.9 %all-reduce.11.cloned.1.call-done = bf16[512,512]{0,1:T(8,128)(2,1)} async-done(((bf16[512,512]{0,1:T(8,128)(2,1)}), bf16[512,512]{0,1:T(8,128)(2,1)}) %all-reduce.11.cloned.1.call-update) | async-done | bytes 524304 | tf_op jit(solution)/shard_map/psum | solution.py:9
  231.4 1.3 copy.4
  232.7 143.8 %all-reduce.9.cloned.1.call-done = bf16[3584,512]{1,0:T(8,128)(2,1)} async-done(((bf16[3584,512]{1,0:T(8,128)(2,1)}), bf16[3584,512]{1,0:T(8,128)(2,1)}) %all-reduce.9.cloned.1.call-update) | async-done | bytes 3670032 | tf_op jit(solution)/shard_map/psum | solution.py:9
  376.5 9.3 %fusion = bf16[3584,512]{1,0:T(8,128)(2,1)} fusion(bf16[3584,512]{1,0:T(8,128)(2,1)} %all-reduce.9.cloned.1.call-done, pred[3584]{0:T(1024)(128)(4,1)S(1)} %get-tuple-element.17, pred[3584]{0:T(1024)(128)(4,1)S(1)} %get-tuple-element.18, bf16[3072,512]{1,0:T(8,128)(2,1)} %copy-done.3, bf16[512,512]{1,0:T(8,128)(2,1)S(1)} %fusion.10, ...), kind=kOutput, calls=%fused_computation.4 | convolution fusion | flops 1895825408 | bytes 11541505 | tf_op jit(solution)/shard_map/dot_general | solution.py:34
  385.8 2.0 fusion.22
  (11 shorter events, 0.1 us)
Async XLA Ops:
  6.5 151.1 %all-reduce.7.cloned.1.call-start = ((), (), s32[]{:S(2)}) async-start(), calls=%async_computation.1 | async-start | bytes 7340032 | tf_op jit(solution)/shard_map/psum | solution.py:9
  15.7 1.6 copy-start
  15.8 177.7 %all-reduce.5.cloned.1.call-start = ((), (), s32[]{:S(2)}) async-start(), calls=%async_computation | async-start | bytes 1048576 | tf_op jit(solution)/shard_map/psum | solution.py:9
  20.2 211.2 %all-reduce.11.cloned.1.call-start = ((), (), s32[]{:S(2)}) async-start(), calls=%async_computation.3 | async-start | bytes 1048576 | tf_op jit(solution)/shard_map/psum | solution.py:9
  193.5 4.5 %copy-start.2 = (bf16[512,512]{1,0:T(8,128)(2,1)S(1)}, bf16[512,512]{1,0:T(8,128)(2,1)}, u32[]{:S(2)}) copy-start(bf16[512,512]{1,0:T(8,128)(2,1)} %all-reduce.5.cloned.1.call-done) | copy-start | bytes 1572868
  197.7 7.7 %copy-start.1 = (f32[2,512,512]{2,1,0:T(8,128)S(1)}, f32[2,512,512]{2,1,0:T(8,128)}, u32[]{:S(2)}) copy-start(f32[2,512,512]{2,1,0:T(8,128)} %param.6) | copy-start | bytes 6291460
  197.8 178.7 %all-reduce.9.cloned.1.call-start = ((), (), s32[]{:S(2)}) async-start(), calls=%async_computation.2 | async-start | bytes 7340032 | tf_op jit(solution)/shard_map/psum | solution.py:9
  203.7 1.7 copy-start.3
Sparse Core Ops, SparseCore 0:
  15.9 141.6 all-reduce.6
  160.0 33.5 all-reduce.4
  197.9 33.5 all-reduce.10
  234.9 141.4 all-reduce.8
where the time goes:
time: 399 us; the launch traced here: 394 us
  waiting for transfers between devices  330 us (83%)
  matrix products  39.3 us (10%)
  between operations  13.2 us (3%)
  other arithmetic  6.56 us (2%)
  local copies, waits for them, and re-layouts  4.46 us (1%)
    psum x4, waiting for transfers between devices, broadcast(): return lax.psum(block, axis)  330 us
    dot_general x2, matrix products, lower_factor(): jnp.dot(panel, u_inverse[panel_id], precision=lax.Precision.HIGHEST)  17.3 us
    dot_general x3, matrix products, apply_update(): product = jnp.dot(lower, upper, preferred_element_type=jnp.float32)  17.2 us
  transfers between devices with their start and end apart: 4, of which 4 were waited for; matrix products, arithmetic and copies ran while one was open for 6% of the time, Pallas kernels for 0%

commit v1 on v0

v1 whole, which is shorter than its diff:
```python
import functools

import jax
import jax.numpy as jnp
from jax import lax
from jax.experimental import pallas as pl
from jax.experimental.pallas import tpu as pltpu
from jax.sharding import PartitionSpec as P

MESH = pl.DeviceIdType.MESH
BF = jnp.bfloat16
F32 = jnp.float32
PER_BLOCK = 8


def dot(a, b):
    return jnp.dot(a, b, preferred_element_type=F32)


def times_upper(a, u_ref, panel):
    half = a.shape[1] // 2
    left = sum(dot(a[:, :half], u_ref[panel, i, :half, :half]) for i in (2, 1, 0))
    right = sum(dot(a, u_ref[panel, i, :, half:]) for i in (2, 1, 0))
    return jnp.concatenate([left, right], 1).astype(BF)


def kernel(
    n_prow, n_pcol, width, m_ref, u_hbm, l_hbm, out_ref,
    own, buf, sbuf, uf, lf, us, ls, ucat, u1, lg1, cg1, low0, low1, cur, fresh, obuf,
    local_sem, recv, fwd, cross, sp_recv, sp_send, out_sem,
):
    rows = own.shape[0]
    chunk = width // PER_BLOCK
    chunks = rows // chunk
    half, blocks = width // 2, rows // width
    first = chunks - 4 * blocks
    prow, pcol = lax.axis_index("prow"), lax.axis_index("pcol")
    q, r = pcol % 2, prow % 2
    qx, rx = 1 - q, 1 - r
    pcol_x, prow_x = pcol + 1 - 2 * q, prow + 1 - 2 * r
    source, last = pcol < 2, pcol + 2 >= n_pcol
    top, bottom = prow < 2, prow + 2 >= n_prow
    special = pl.ds(rows, width)

    load_own = pltpu.make_async_copy(m_ref, own, local_sem.at[0])
    load_u = pltpu.make_async_copy(u_hbm, uf, local_sem.at[1])
    load_l = pltpu.make_async_copy(l_hbm, lf, local_sem.at[2])
    load_stream = pltpu.make_async_copy(m_ref, buf.at[q, pl.ds(0, rows)], local_sem.at[3])
    load_special = pltpu.make_async_copy(
        m_ref.at[pl.ds(0, width)], buf.at[q, special], local_sem.at[4]
    )
    load_head = pltpu.make_async_copy(m_ref.at[pl.ds(0, width)], sbuf.at[r], local_sem.at[5])
    source_special = source & (prow == qx)

    @pl.when(source)
    def _():
        load_stream.start()

    @pl.when(source_special)
    def _():
        load_special.start()

    @pl.when(top)
    def _():
        load_head.start()

    load_u.start()
    load_l.start()
    load_own.start()

    barrier = pltpu.get_barrier_semaphore()

    def greet(where):
        pl.semaphore_signal(barrier, inc=1, device_id=where, device_id_type=MESH)

    greet({"pcol": pcol_x})
    greet({"prow": prow_x})
    for ok, where in (
        (jnp.logical_not(source), {"pcol": pcol - 2}),
        (jnp.logical_not(last), {"pcol": pcol + 2}),
        (jnp.logical_not(top), {"prow": prow - 2}),
        (jnp.logical_not(bottom), {"prow": prow + 2}),
    ):
        pl.when(ok)(functools.partial(greet, where))
    absent = [jnp.where(ok, 1, 0) for ok in (source, last, top, bottom)]
    pl.semaphore_wait(barrier, 6 - sum(absent))

    def place(stream, k):
        shift = jnp.where((prow == 1 - stream) & (k < PER_BLOCK), rows, 0)
        at = pl.multiple_of(shift + k * chunk, chunk)
        return buf.at[stream, pl.ds(at, chunk)], (prow != stream) | (k >= PER_BLOCK)

    def stream_copy(stream, k, send_sem, where):
        ref, _ = place(stream, k)
        return pltpu.make_async_remote_copy(
            src_ref=ref, dst_ref=ref, send_sem=send_sem.at[k], recv_sem=recv.at[stream, k],
            device_id={"pcol": where}, device_id_type=MESH,
        )

    def send(k):
        @pl.when(jnp.logical_not(last))
        def _():
            stream_copy(q, k, fwd, pcol + 2).start()

        stream_copy(q, k, cross, pcol_x).start()

    def relay(k):
        @pl.when(jnp.logical_not(source) & place(q, k)[1])
        def _():
            stream_copy(q, k, fwd, pcol_x).wait_recv()
            send(k)

    def arrive(k):
        @pl.when(place(qx, k)[1])
        def _():
            stream_copy(qx, k, fwd, pcol_x).wait_recv()

    def loop(lo, hi, step):
        def one(k, carry):
            step(k)
            return carry

        lax.fori_loop(lo, hi, one, 0)

    def special_copy(which, across):
        ref = sbuf.at[r] if which == 0 else buf.at[rx, special]
        i = which + 2 * across
        return pltpu.make_async_remote_copy(
            src_ref=ref, dst_ref=ref, send_sem=sp_send.at[i], recv_sem=sp_recv.at[i],
            device_id={"prow": prow_x if across else prow + 2}, device_id_type=MESH,
        )

    def arrived_special(which, across):
        mine = rx if across else r
        ref = sbuf.at[mine] if which == 0 else buf.at[1 - mine, special]
        i = which + 2 * across
        pltpu.make_async_remote_copy(
            src_ref=ref, dst_ref=ref, send_sem=sp_send.at[i], recv_sem=sp_recv.at[i],
            device_id={"prow": prow_x}, device_id_type=MESH,
        ).wait_recv()

    def pass_special(which):
        @pl.when(jnp.logical_not(bottom))
        def _():
            special_copy(which, 0).start()

        special_copy(which, 1).start()

    @pl.when(top)
    def _():
        load_head.wait()
        pass_special(0)

    @pl.when(source_special)
    def _():
        load_special.wait()

    @pl.when(source)
    def _():
        load_stream.wait()
        loop(jnp.where(prow == q, PER_BLOCK, 0), chunks, send)

    load_u.wait()
    load_l.wait()
    load_own.wait()

    def split(src, dst, panel):
        rest = src[panel]
        for i in range(3):
            piece = rest.astype(BF)
            dst[panel, i] = piece
            rest = rest - piece.astype(F32)

    for n, (src, dst, panel) in enumerate(((lf, ls, 0), (uf, us, 0), (lf, ls, 1), (uf, us, 1))):
        split(src, dst, panel)
        relay(n)
    loop(4, PER_BLOCK, relay)

    @pl.when(top)
    def _():
        pl.when(q == r)(functools.partial(loop, 0, PER_BLOCK, arrive))
        pass_special(1)

    loop(PER_BLOCK, 2 * PER_BLOCK, relay)

    @pl.when(jnp.logical_not(top))
    def _():
        arrived_special(0, 0)
        pass_special(0)

    loop(2 * PER_BLOCK, first - 4, relay)

    @pl.when(jnp.logical_not(top))
    def _():
        arrived_special(1, 0)
        pass_special(1)

    loop(first - 4, first, relay)

    arrived_special(0, 1)
    arrived_special(1, 1)

    def lower_times(panel, value, out, at):
        upper = sum(dot(ls[panel, i, :half, :half], value[:half]) for i in (2, 1, 0))
        lower = sum(dot(ls[panel, i, half:], value) for i in (2, 1, 0))
        out[:half, at] = upper.astype(BF)
        out[half:, at] = lower.astype(BF)

    whole = slice(0, width)
    lower_times(0, buf[1, special], ucat, whole)
    relay(first)
    lower_times(0, sbuf[0], ucat, slice(width, 2 * width))
    relay(first + 1)
    lg1[...] = times_upper(buf[0, special], us, 0)
    relay(first + 2)
    cg1[...] = (sbuf[1].astype(F32) - dot(lg1[...], ucat[:, width:])).astype(BF)
    relay(first + 3)
    lower_times(1, cg1[...], u1, whole)

    def store(at, n, value, sem):
        obuf[pl.ds(at, n)] = value
        pltpu.make_async_copy(obuf.at[pl.ds(at, n)], out_ref.at[pl.ds(at, n)], sem).start()

    @pl.when(prow == 0)
    def _():
        store(0, width, jnp.where(pcol == 0, own[:width], ucat[:, width:]), out_sem.at[0])

    @pl.when(prow == 1)
    def _():
        value = jnp.where(pcol == 1, cg1[...], u1[...])
        store(0, width, jnp.where(pcol == 0, lg1[...], value), out_sem.at[0])

    def block(at, n, sem, between, active):
        at = pl.multiple_of(at, n)
        here, part = pl.ds(at, n), pl.ds(0, n)

        @pl.when(active)
        def _():
            low0[part] = times_upper(buf[0, here], us, 0)

        between(0)

        @pl.when(active)
        def _():
            a = dot(low0[part], ucat[...])
            cur[part] = (buf[1, here].astype(F32) - a[:, :width]).astype(BF)
            fresh[part] = (own[here].astype(F32) - a[:, width:]).astype(BF)

        between(1)

        @pl.when(active)
        def _():
            low1[part] = times_upper(cur[part], us, 1)

        between(2)

        @pl.when(active)
        def _():
            value = (fresh[part].astype(F32) - dot(low1[part], u1[...])).astype(BF)
            value = jnp.where(pcol == 1, low1[part], value)
            store(at, n, jnp.where(pcol == 0, low0[part], value), sem)

        between(3)

    def steps(b, slot):
        relay(first + 4 + b * 4 + slot)

    def one_block(b, carry):
        skip = (b == 0) & top

        @pl.when(jnp.logical_not(skip & (q == r)))
        def _():
            loop(b * PER_BLOCK, (b + 1) * PER_BLOCK, arrive)

        block(
            b * width, width, out_sem.at[b], functools.partial(steps, b), jnp.logical_not(skip)
        )
        return carry

    lax.fori_loop(0, blocks - 1, one_block, 0)
    for n in range(2):
        lo = (blocks - 1) * PER_BLOCK + n * (PER_BLOCK // 2)
        loop(lo, lo + PER_BLOCK // 2, arrive)
        block(lo * chunk, half, out_sem.at[blocks - 1 + n], lambda slot: None, True)

    for i in range(4):
        if i < 2:
            pl.when(jnp.logical_not(bottom))(special_copy(i, 0).wait_send)
        else:
            special_copy(i - 2, 1).wait_send()

    def sent(k):
        pl.when(jnp.logical_not(last))(lambda: stream_copy(q, k, fwd, pcol_x).wait_send())
        stream_copy(q, k, cross, pcol_x).wait_send()

    loop(jnp.where(prow == q, PER_BLOCK, 0), chunks, sent)

    def written(at, n, sem):
        pltpu.make_async_copy(obuf.at[pl.ds(at, n)], out_ref.at[pl.ds(at, n)], sem).wait()

    loop(0, blocks - 1, lambda b: written(pl.multiple_of(b * width, width), width, out_sem.at[b]))
    for n in range(2):
        written(rows - width + n * half, half, out_sem.at[blocks - 1 + n])


def body(n_prow, n_pcol, matrix, u_inverse, l_inverse):
    rows, width = matrix.shape
    chunks = rows // (width // PER_BLOCK)
    square = (width, width)
    dma = pltpu.SemaphoreType.DMA
    return pl.pallas_call(
        functools.partial(kernel, n_prow, n_pcol, width),
        out_shape=jax.ShapeDtypeStruct(matrix.shape, matrix.dtype),
        in_specs=[pl.BlockSpec(memory_space=pl.ANY)] * 3,
        out_specs=pl.BlockSpec(memory_space=pl.ANY),
        scratch_shapes=[
            pltpu.VMEM((rows, width), BF),
            pltpu.VMEM((2, rows + width, width), BF),
            pltpu.VMEM((2,) + square, BF),
            pltpu.VMEM((2,) + square, F32),
            pltpu.VMEM((2,) + square, F32),
            pltpu.VMEM((2, 3) + square, BF),
            pltpu.VMEM((2, 3) + square, BF),
            pltpu.VMEM((width, 2 * width), BF),
        ]
        + [pltpu.VMEM(square, BF)] * 7
        + [
            pltpu.VMEM((rows, width), BF),
            dma((6,)),
            dma((2, chunks)),
            dma((chunks,)),
            dma((chunks,)),
            dma((4,)),
            dma((4,)),
            dma((rows // width + 1,)),
        ],
        compiler_params=pltpu.CompilerParams(
            collective_id=0, has_side_effects=True, vmem_limit_bytes=60 * 1024 * 1024
        ),
    )(matrix, u_inverse, l_inverse)


def solution(mesh):
    run = functools.partial(body, mesh.shape["prow"], mesh.shape["pcol"])
    in_specs = (P("prow", "pcol"), P(), P())
    out_specs = P("prow", "pcol")
    return jax.shard_map(run, mesh=mesh, in_specs=in_specs, out_specs=out_specs, check_vma=False)
```

time: 399 us -> 103 us (0.26)
  waiting for transfers between devices: 330 us -> 0 us
  Pallas kernels: 0 us -> 96.5 us
  matrix products: 39.3 us -> 0 us
  between operations: 13.2 us -> 0.01 us
  other arithmetic: 6.56 us -> 0 us
    psum x4 -> x0, waiting for transfers between devices: 330 us -> none  [broadcast(): return lax.psum(block, axis)]
    pallas_call x0 -> x1, Pallas kernels: none -> 96.5 us  [body(): pl.pallas_call(functools.partial(kernel, n_prow, n_pcol, width), out_shap...]
    dot_general x7 -> x0, matrix products: 39.3 us -> none  [the longest x2 17.3 us: lower_factor(): jnp.dot(panel, u_inverse[panel_id], precision=lax.Precision.HIGHEST)]
    select_n x1 -> x0, other arithmetic: 4.53 us -> none  [lower_factor(): return jnp.where(row_ids[:, None] > panel_id, lower, jnp.zeros_like(lower))]
  transfers between devices with their start and end apart: 4 -> 0, of which waited for: 4 -> 0; matrix products, arithmetic and copies ran while one was open for 6% -> 0% of each run, Pallas kernels for 0% -> 0%
where the time goes in v1:
time: 103 us; the launch traced here: 101 us
  Pallas kernels  96.5 us (94%)
  local copies, waits for them, and re-layouts  4.11 us (4%)
    pallas_call x1, Pallas kernels, body(): pl.pallas_call(functools.partial(kernel, n_prow, n_pcol, width), out_shap...  96.5 us
    unnamed x1, local copies, waits for them, and re-layouts  4.11 us

profile of v1, /device:TPU:28, one launch (start us, length us, event | category | flops | bytes accessed | tf_op | source)
XLA Modules:
  0.0 100.6 jit_solution(1055177312017848485)
XLA Ops:
  0.0 96.5 %shard_map.37 = bf16[3584,512]{1,0:T(8,128)(2,1)} custom-call(bf16[3584,512]{1,0:T(8,128)(2,1)} %m_ref.1, f32[2,512,512]{2,1,0:T(8,128)} %u_hbm.1, f32[2,512,512]{2,1,0:T(8,128)} %l_hbm.1), custom_call_target="tpu_custom_call" | custom-call | tf_op jit(solution)/shard_map/pallas_call | solution.py:311
  96.5 4.1 %copy.5 = bf16[3584,512]{1,0:T(8,128)(2,1)} copy(bf16[3584,512]{1,0:T(8,128)(2,1)} %shard_map.37) | data formatting | bytes 7340032

commit v2 on v1

--- a/solution.py
+++ b/solution.py
@@ -10,7 +10,7 @@
 MESH = pl.DeviceIdType.MESH
 BF = jnp.bfloat16
 F32 = jnp.float32
-PER_BLOCK = 8
+PER_BLOCK = 16
 
 
 def dot(a, b):
@@ -33,7 +33,7 @@
     chunk = width // PER_BLOCK
     chunks = rows // chunk
     half, blocks = width // 2, rows // width
-    first = chunks - 4 * blocks
+    first = chunks - 4 * (2 * blocks - 1)
     prow, pcol = lax.axis_index("prow"), lax.axis_index("pcol")
     q, r = pcol % 2, prow % 2
     qx, rx = 1 - q, 1 - r
@@ -104,8 +104,12 @@
 
         stream_copy(q, k, cross, pcol_x).start()
 
-    def relay(k):
-        @pl.when(jnp.logical_not(source) & place(q, k)[1])
+    ahead = jnp.where(prow == q, PER_BLOCK, 0)
+
+    def relay(slot):
+        k = slot + ahead
+
+        @pl.when(jnp.logical_not(source) & (k < chunks))
         def _():
             stream_copy(q, k, fwd, pcol_x).wait_recv()
             send(k)
@@ -158,7 +162,7 @@
     @pl.when(source)
     def _():
         load_stream.wait()
-        loop(jnp.where(prow == q, PER_BLOCK, 0), chunks, send)
+        loop(ahead, chunks, send)
 
     load_u.wait()
     load_l.wait()
@@ -174,48 +178,47 @@
     for n, (src, dst, panel) in enumerate(((lf, ls, 0), (uf, us, 0), (lf, ls, 1), (uf, us, 1))):
         split(src, dst, panel)
         relay(n)
-    loop(4, PER_BLOCK, relay)
+    loop(4, PER_BLOCK + 2, relay)
 
     @pl.when(top)
     def _():
         pl.when(q == r)(functools.partial(loop, 0, PER_BLOCK, arrive))
         pass_special(1)
 
-    loop(PER_BLOCK, 2 * PER_BLOCK, relay)
+    loop(PER_BLOCK + 2, 2 * PER_BLOCK, relay)
 
     @pl.when(jnp.logical_not(top))
     def _():
         arrived_special(0, 0)
         pass_special(0)
 
-    loop(2 * PER_BLOCK, first - 4, relay)
+    loop(2 * PER_BLOCK, first - 16, relay)
 
     @pl.when(jnp.logical_not(top))
     def _():
         arrived_special(1, 0)
         pass_special(1)
 
-    loop(first - 4, first, relay)
-
+    loop(first - 16, first - 8, relay)
     arrived_special(0, 1)
     arrived_special(1, 1)
 
-    def lower_times(panel, value, out, at):
+    def lower_times(panel, value, out, at, slot):
         upper = sum(dot(ls[panel, i, :half, :half], value[:half]) for i in (2, 1, 0))
+        out[:half, at] = upper.astype(BF)
+        relay(slot)
         lower = sum(dot(ls[panel, i, half:], value) for i in (2, 1, 0))
-        out[:half, at] = upper.astype(BF)
         out[half:, at] = lower.astype(BF)
+        relay(slot + 1)
 
     whole = slice(0, width)
-    lower_times(0, buf[1, special], ucat, whole)
-    relay(first)
-    lower_times(0, sbuf[0], ucat, slice(width, 2 * width))
-    relay(first + 1)
+    lower_times(0, buf[1, special], ucat, whole, first - 8)
+    lower_times(0, sbuf[0], ucat, slice(width, 2 * width), first - 6)
     lg1[...] = times_upper(buf[0, special], us, 0)
-    relay(first + 2)
+    relay(first - 4)
     cg1[...] = (sbuf[1].astype(F32) - dot(lg1[...], ucat[:, width:])).astype(BF)
-    relay(first + 3)
-    lower_times(1, cg1[...], u1, whole)
+    relay(first - 3)
+    lower_times(1, cg1[...], u1, whole, first - 2)
 
     def store(at, n, value, sem):
         obuf[pl.ds(at, n)] = value
@@ -262,26 +265,30 @@
 
         between(3)
 
-    def steps(b, slot):
-        relay(first + 4 + b * 4 + slot)
-
-    def one_block(b, carry):
-        skip = (b == 0) & top
+    tiles = 2 * blocks - 1
+
+    def one_tile(t, carry):
+        skip = (t < 2) & top
 
         @pl.when(jnp.logical_not(skip & (q == r)))
         def _():
-            loop(b * PER_BLOCK, (b + 1) * PER_BLOCK, arrive)
+            loop(t * (PER_BLOCK // 2), (t + 1) * (PER_BLOCK // 2), arrive)
 
         block(
-            b * width, width, out_sem.at[b], functools.partial(steps, b), jnp.logical_not(skip)
+            t * half,
+            half,
+            out_sem.at[1 + t],
+            lambda slot: relay(first + 4 * t + slot),
+            jnp.logical_not(skip),
         )
         return carry
 
-    lax.fori_loop(0, blocks - 1, one_block, 0)
+    lax.fori_loop(0, tiles, one_tile, 0)
+    quarter = half // 2
     for n in range(2):
-        lo = (blocks - 1) * PER_BLOCK + n * (PER_BLOCK // 2)
-        loop(lo, lo + PER_BLOCK // 2, arrive)
-        block(lo * chunk, half, out_sem.at[blocks - 1 + n], lambda slot: None, True)
+        lo = tiles * (PER_BLOCK // 2) + n * (PER_BLOCK // 4)
+        loop(lo, lo + PER_BLOCK // 4, arrive)
+        block(lo * chunk, quarter, out_sem.at[1 + tiles + n], lambda slot: None, True)
 
     for i in range(4):
         if i < 2:
@@ -293,14 +300,19 @@
         pl.when(jnp.logical_not(last))(lambda: stream_copy(q, k, fwd, pcol_x).wait_send())
         stream_copy(q, k, cross, pcol_x).wait_send()
 
-    loop(jnp.where(prow == q, PER_BLOCK, 0), chunks, sent)
+    loop(ahead, chunks, sent)
 
     def written(at, n, sem):
         pltpu.make_async_copy(obuf.at[pl.ds(at, n)], out_ref.at[pl.ds(at, n)], sem).wait()
 
-    loop(0, blocks - 1, lambda b: written(pl.multiple_of(b * width, width), width, out_sem.at[b]))
+    pl.when(top)(lambda: written(0, width, out_sem.at[0]))
+    loop(
+        jnp.where(top, 2, 0),
+        tiles,
+        lambda t: written(pl.multiple_of(t * half, half), half, out_sem.at[1 + t]),
+    )
     for n in range(2):
-        written(rows - width + n * half, half, out_sem.at[blocks - 1 + n])
+        written(rows - half + n * quarter, quarter, out_sem.at[1 + tiles + n])
 
 
 def body(n_prow, n_pcol, matrix, u_inverse, l_inverse):
@@ -311,7 +323,7 @@
     return pl.pallas_call(
         functools.partial(kernel, n_prow, n_pcol, width),
         out_shape=jax.ShapeDtypeStruct(matrix.shape, matrix.dtype),
-        in_specs=[pl.BlockSpec(memory_space=pl.ANY)] * 3,
+        in_specs=[pl.BlockSpec(memory_space=pltpu.HBM)] * 3,
         out_specs=pl.BlockSpec(memory_space=pl.ANY),
         scratch_shapes=[
             pltpu.VMEM((rows, width), BF),
@@ -332,10 +344,10 @@
             dma((chunks,)),
             dma((4,)),
             dma((4,)),
-            dma((rows // width + 1,)),
+            dma((2 * rows // width + 2,)),
         ],
         compiler_params=pltpu.CompilerParams(
-            collective_id=0, has_side_effects=True, vmem_limit_bytes=60 * 1024 * 1024
+            collective_id=0, has_side_effects=True, vmem_limit_bytes=56 * 1024 * 1024
         ),
     )(matrix, u_inverse, l_inverse)
 

time: 103 us -> 101 us (0.981); the launches traced: 101 us -> 101 us
  no operation moved by 1% of the time
where the time goes in v2:
time: 101 us
  Pallas kernels  97.2 us (96%)
  local copies, waits for them, and re-layouts  4.11 us (4%)
    pallas_call x1, Pallas kernels, body(): pl.pallas_call(functools.partial(kernel, n_prow, n_pcol, width), out_shap...  97.2 us
    unnamed x1, local copies, waits for them, and re-layouts  4.11 us

profile of v2, /device:TPU:28, one launch (start us, length us, event | category | flops | bytes accessed | tf_op | source)
XLA Modules:
  0.0 101.4 jit_solution(5581508070354857331)
XLA Ops:
  0.0 97.2 %shard_map.37 = bf16[3584,512]{1,0:T(8,128)(2,1)} custom-call(bf16[3584,512]{1,0:T(8,128)(2,1)} %m_ref.1, f32[2,512,512]{2,1,0:T(8,128)} %u_hbm.1, f32[2,512,512]{2,1,0:T(8,128)} %l_hbm.1), custom_call_target="tpu_custom_call" | custom-call | tf_op jit(solution)/shard_map/pallas_call | solution.py:323
  97.2 4.1 %copy.5 = bf16[3584,512]{1,0:T(8,128)(2,1)} copy(bf16[3584,512]{1,0:T(8,128)(2,1)} %shard_map.37) | data formatting | bytes 7340032

commit v3 on v2

--- a/solution.py
+++ b/solution.py
@@ -90,19 +90,22 @@
         at = pl.multiple_of(shift + k * chunk, chunk)
         return buf.at[stream, pl.ds(at, chunk)], (prow != stream) | (k >= PER_BLOCK)
 
-    def stream_copy(stream, k, send_sem, where):
+    def stream_copy(stream, k, send_sem, where, src=None):
         ref, _ = place(stream, k)
         return pltpu.make_async_remote_copy(
-            src_ref=ref, dst_ref=ref, send_sem=send_sem.at[k], recv_sem=recv.at[stream, k],
+            src_ref=ref if src is None else src, dst_ref=ref, send_sem=send_sem.at[k], recv_sem=recv.at[stream, k],
             device_id={"pcol": where}, device_id_type=MESH,
         )
 
-    def send(k):
+    def send(k, src=None):
         @pl.when(jnp.logical_not(last))
         def _():
-            stream_copy(q, k, fwd, pcol + 2).start()
-
-        stream_copy(q, k, cross, pcol_x).start()
+            stream_copy(q, k, fwd, pcol + 2, src).start()
+
+        stream_copy(q, k, cross, pcol_x, src).start()
+
+    def send_own(k):
+        send(k, m_ref.at[pl.ds(pl.multiple_of(k * chunk, chunk), chunk)])
 
     ahead = jnp.where(prow == q, PER_BLOCK, 0)
 
@@ -150,6 +153,10 @@
 
         special_copy(which, 1).start()
 
+    @pl.when(source)
+    def _():
+        loop(ahead, chunks, send_own)
+
     @pl.when(top)
     def _():
         load_head.wait()
@@ -159,11 +166,8 @@
     def _():
         load_special.wait()
 
-    @pl.when(source)
-    def _():
-        load_stream.wait()
-        loop(ahead, chunks, send)
-
+    loop(0, 6, relay)
+    pl.when(source)(load_stream.wait)
     load_u.wait()
     load_l.wait()
     load_own.wait()
@@ -177,8 +181,8 @@
 
     for n, (src, dst, panel) in enumerate(((lf, ls, 0), (uf, us, 0), (lf, ls, 1), (uf, us, 1))):
         split(src, dst, panel)
-        relay(n)
-    loop(4, PER_BLOCK + 2, relay)
+        relay(6 + n)
+    loop(10, PER_BLOCK + 2, relay)
 
     @pl.when(top)
     def _():
@@ -284,23 +288,25 @@
         return carry
 
     lax.fori_loop(0, tiles, one_tile, 0)
+    for i in range(4):
+        if i < 2:
+            pl.when(jnp.logical_not(bottom))(special_copy(i, 0).wait_send)
+        else:
+            special_copy(i - 2, 1).wait_send()
+
+    def sent(k):
+        pl.when(jnp.logical_not(last))(lambda: stream_copy(q, k, fwd, pcol_x).wait_send())
+        stream_copy(q, k, cross, pcol_x).wait_send()
+
+    late = chunks - PER_BLOCK // 2
+    loop(ahead, late, sent)
     quarter = half // 2
     for n in range(2):
         lo = tiles * (PER_BLOCK // 2) + n * (PER_BLOCK // 4)
         loop(lo, lo + PER_BLOCK // 4, arrive)
         block(lo * chunk, quarter, out_sem.at[1 + tiles + n], lambda slot: None, True)
 
-    for i in range(4):
-        if i < 2:
-            pl.when(jnp.logical_not(bottom))(special_copy(i, 0).wait_send)
-        else:
-            special_copy(i - 2, 1).wait_send()
-
-    def sent(k):
-        pl.when(jnp.logical_not(last))(lambda: stream_copy(q, k, fwd, pcol_x).wait_send())
-        stream_copy(q, k, cross, pcol_x).wait_send()
-
-    loop(ahead, chunks, sent)
+    loop(late, chunks, sent)
 
     def written(at, n, sem):
         pltpu.make_async_copy(obuf.at[pl.ds(at, n)], out_ref.at[pl.ds(at, n)], sem).wait()
@@ -320,6 +326,9 @@
     chunks = rows // (width // PER_BLOCK)
     square = (width, width)
     dma = pltpu.SemaphoreType.DMA
+    operands = [
+        pltpu.with_memory_space_constraint(x, pltpu.HBM) for x in (matrix, u_inverse, l_inverse)
+    ]
     return pl.pallas_call(
         functools.partial(kernel, n_prow, n_pcol, width),
         out_shape=jax.ShapeDtypeStruct(matrix.shape, matrix.dtype),
@@ -347,9 +356,9 @@
             dma((2 * rows // width + 2,)),
         ],
         compiler_params=pltpu.CompilerParams(
-            collective_id=0, has_side_effects=True, vmem_limit_bytes=56 * 1024 * 1024
+            collective_id=0, has_side_effects=True, vmem_limit_bytes=46 * 1024 * 1024
         ),
-    )(matrix, u_inverse, l_inverse)
+    )(*operands)
 
 
 def solution(mesh):

time: 101 us -> 98.4 us (0.974)
  local copies, waits for them, and re-layouts: 4.11 us -> 1.84 us
    unnamed x1, local copies, waits for them, and re-layouts: 4.11 us -> 1.84 us
where the time goes in v3:
time: 98.4 us; the launch traced here: 98.1 us
  Pallas kernels  96.2 us (98%)
  local copies, waits for them, and re-layouts  1.84 us (2%)
    pallas_call x1, Pallas kernels, body(): pl.pallas_call(functools.partial(kernel, n_prow, n_pcol, width), out_shap...  96.2 us

profile of v3, /device:TPU:28, one launch (start us, length us, event | category | flops | bytes accessed | tf_op | source)
XLA Modules:
  0.0 98.1 jit_solution(11828326195622183070)
XLA Ops:
  0.0 96.2 %shard_map.37 = bf16[3584,512]{1,0:T(8,128)(2,1)S(1)} custom-call(bf16[3584,512]{1,0:T(8,128)(2,1)} %m_ref.1, f32[2,512,512]{2,1,0:T(8,128)} %u_hbm.1, f32[2,512,512]{2,1,0:T(8,128)} %l_hbm.1), custom_call_target="tpu_custom_call" | custom-call | tf_op jit(solution)/shard_map/pallas_call | solution.py:332
  96.2 1.8 %copy.5 = bf16[3584,512]{1,0:T(8,128)(2,1)} copy(bf16[3584,512]{1,0:T(8,128)(2,1)S(1)} %shard_map.37) | data formatting | bytes 7340032

commit v4 on v3

--- a/solution.py
+++ b/solution.py
@@ -11,6 +11,7 @@
 BF = jnp.bfloat16
 F32 = jnp.float32
 PER_BLOCK = 16
+PIECES = 2
 
 
 def dot(a, b):
@@ -19,8 +20,8 @@
 
 def times_upper(a, u_ref, panel):
     half = a.shape[1] // 2
-    left = sum(dot(a[:, :half], u_ref[panel, i, :half, :half]) for i in (2, 1, 0))
-    right = sum(dot(a, u_ref[panel, i, :, half:]) for i in (2, 1, 0))
+    left = sum(dot(a[:, :half], u_ref[panel, i, :half, :half]) for i in reversed(range(PIECES)))
+    right = sum(dot(a, u_ref[panel, i, :, half:]) for i in reversed(range(PIECES)))
     return jnp.concatenate([left, right], 1).astype(BF)
 
 
@@ -174,7 +175,7 @@
 
     def split(src, dst, panel):
         rest = src[panel]
-        for i in range(3):
+        for i in range(PIECES):
             piece = rest.astype(BF)
             dst[panel, i] = piece
             rest = rest - piece.astype(F32)
@@ -208,10 +209,10 @@
     arrived_special(1, 1)
 
     def lower_times(panel, value, out, at, slot):
-        upper = sum(dot(ls[panel, i, :half, :half], value[:half]) for i in (2, 1, 0))
+        upper = sum(dot(ls[panel, i, :half, :half], value[:half]) for i in reversed(range(PIECES)))
         out[:half, at] = upper.astype(BF)
         relay(slot)
-        lower = sum(dot(ls[panel, i, half:], value) for i in (2, 1, 0))
+        lower = sum(dot(ls[panel, i, half:], value) for i in reversed(range(PIECES)))
         out[half:, at] = lower.astype(BF)
         relay(slot + 1)
 
@@ -271,23 +272,31 @@
 
     tiles = 2 * blocks - 1
 
-    def one_tile(t, carry):
+    def one_tile(t, between):
         skip = (t < 2) & top
 
         @pl.when(jnp.logical_not(skip & (q == r)))
         def _():
             loop(t * (PER_BLOCK // 2), (t + 1) * (PER_BLOCK // 2), arrive)
 
-        block(
-            t * half,
-            half,
-            out_sem.at[1 + t],
-            lambda slot: relay(first + 4 * t + slot),
-            jnp.logical_not(skip),
-        )
-        return carry
-
-    lax.fori_loop(0, tiles, one_tile, 0)
+        block(t * half, half, out_sem.at[1 + t], between, jnp.logical_not(skip))
+
+    def nothing(slot):
+        pass
+
+    loop(0, tiles - 1, lambda t: one_tile(t, lambda slot: relay(first + 4 * t + slot)))
+    loop(first + 4 * (tiles - 1), chunks, relay)
+    one_tile(tiles - 1, nothing)
+
+    quarter = half // 2
+
+    def one_quarter(n):
+        lo = tiles * (PER_BLOCK // 2) + n * (PER_BLOCK // 4)
+        loop(lo, lo + PER_BLOCK // 4, arrive)
+        block(lo * chunk, quarter, out_sem.at[1 + tiles + n], nothing, True)
+
+    one_quarter(0)
+
     for i in range(4):
         if i < 2:
             pl.when(jnp.logical_not(bottom))(special_copy(i, 0).wait_send)
@@ -300,11 +309,7 @@
 
     late = chunks - PER_BLOCK // 2
     loop(ahead, late, sent)
-    quarter = half // 2
-    for n in range(2):
-        lo = tiles * (PER_BLOCK // 2) + n * (PER_BLOCK // 4)
-        loop(lo, lo + PER_BLOCK // 4, arrive)
-        block(lo * chunk, quarter, out_sem.at[1 + tiles + n], lambda slot: None, True)
+    one_quarter(1)
 
     loop(late, chunks, sent)
 
@@ -340,8 +345,8 @@
             pltpu.VMEM((2,) + square, BF),
             pltpu.VMEM((2,) + square, F32),
             pltpu.VMEM((2,) + square, F32),
-            pltpu.VMEM((2, 3) + square, BF),
-            pltpu.VMEM((2, 3) + square, BF),
+            pltpu.VMEM((2, PIECES) + square, BF),
+            pltpu.VMEM((2, PIECES) + square, BF),
             pltpu.VMEM((width, 2 * width), BF),
         ]
         + [pltpu.VMEM(square, BF)] * 7

time: 98.4 us -> 97.5 us (level)
  no operation moved by 1% of the time
where the time goes in v4:
time: 97.5 us; the launch traced here: 97.3 us
  Pallas kernels  95.5 us (98%)
  local copies, waits for them, and re-layouts  1.84 us (2%)
    pallas_call x1, Pallas kernels, body(): pl.pallas_call(functools.partial(kernel, n_prow, n_pcol, width), out_shap...  95.5 us

profile of v4, /device:TPU:28, one launch (start us, length us, event | category | flops | bytes accessed | tf_op | source)
XLA Modules:
  0.0 97.3 jit_solution(11708628154613121217)
XLA Ops:
  0.0 95.5 %shard_map.37 = bf16[3584,512]{1,0:T(8,128)(2,1)S(1)} custom-call(bf16[3584,512]{1,0:T(8,128)(2,1)} %m_ref.1, f32[2,512,512]{2,1,0:T(8,128)} %u_hbm.1, f32[2,512,512]{2,1,0:T(8,128)} %l_hbm.1), custom_call_target="tpu_custom_call" | custom-call | tf_op jit(solution)/shard_map/pallas_call | solution.py:337
  95.5 1.8 %copy.5 = bf16[3584,512]{1,0:T(8,128)(2,1)} copy(bf16[3584,512]{1,0:T(8,128)(2,1)S(1)} %shard_map.37) | data formatting | bytes 7340032

commit v5 on v4

--- a/solution.py
+++ b/solution.py
@@ -10,8 +10,9 @@
 MESH = pl.DeviceIdType.MESH
 BF = jnp.bfloat16
 F32 = jnp.float32
-PER_BLOCK = 16
-PIECES = 2
+PER_BLOCK = 32
+STEP = 2
+PIECES = 3
 
 
 def dot(a, b):
@@ -34,7 +35,8 @@
     chunk = width // PER_BLOCK
     chunks = rows // chunk
     half, blocks = width // 2, rows // width
-    first = chunks - 4 * (2 * blocks - 1)
+    places = chunks // STEP
+    first = places - 4 * (2 * blocks - 1)
     prow, pcol = lax.axis_index("prow"), lax.axis_index("pcol")
     q, r = pcol % 2, prow % 2
     qx, rx = 1 - q, 1 - r
@@ -111,12 +113,13 @@
     ahead = jnp.where(prow == q, PER_BLOCK, 0)
 
     def relay(slot):
-        k = slot + ahead
+        k = slot * STEP + ahead
 
         @pl.when(jnp.logical_not(source) & (k < chunks))
         def _():
-            stream_copy(q, k, fwd, pcol_x).wait_recv()
-            send(k)
+            for i in range(STEP):
+                stream_copy(q, k + i, fwd, pcol_x).wait_recv()
+                send(k + i)
 
     def arrive(k):
         @pl.when(place(qx, k)[1])
@@ -183,21 +186,21 @@
     for n, (src, dst, panel) in enumerate(((lf, ls, 0), (uf, us, 0), (lf, ls, 1), (uf, us, 1))):
         split(src, dst, panel)
         relay(6 + n)
-    loop(10, PER_BLOCK + 2, relay)
+    loop(10, PER_BLOCK // STEP + 2, relay)
 
     @pl.when(top)
     def _():
         pl.when(q == r)(functools.partial(loop, 0, PER_BLOCK, arrive))
         pass_special(1)
 
-    loop(PER_BLOCK + 2, 2 * PER_BLOCK, relay)
+    loop(PER_BLOCK // STEP + 2, 2 * PER_BLOCK // STEP, relay)
 
     @pl.when(jnp.logical_not(top))
     def _():
         arrived_special(0, 0)
         pass_special(0)
 
-    loop(2 * PER_BLOCK, first - 16, relay)
+    loop(2 * PER_BLOCK // STEP, first - 16, relay)
 
     @pl.when(jnp.logical_not(top))
     def _():
@@ -285,7 +288,7 @@
         pass
 
     loop(0, tiles - 1, lambda t: one_tile(t, lambda slot: relay(first + 4 * t + slot)))
-    loop(first + 4 * (tiles - 1), chunks, relay)
+    loop(first + 4 * (tiles - 1), places, relay)
     one_tile(tiles - 1, nothing)
 
     quarter = half // 2

time: 97.5 us -> 103 us (1.056)
  Pallas kernels: 95.5 us -> 101 us
    pallas_call x1, Pallas kernels: 95.5 us -> 101 us  [body(): pl.pallas_call(functools.partial(kernel, n_prow, n_pcol, width), out_shap...]
where the time goes in v5:
time: 103 us
  Pallas kernels  101 us (98%)
  local copies, waits for them, and re-layouts  1.84 us (2%)
    pallas_call x1, Pallas kernels, body(): pl.pallas_call(functools.partial(kernel, n_prow, n_pcol, width), out_shap...  101 us

profile of v5, /device:TPU:28, one launch (start us, length us, event | category | flops | bytes accessed | tf_op | source)
XLA Modules:
  0.0 103.1 jit_solution(14384661423046717794)
XLA Ops:
  0.0 101.2 %shard_map.37 = bf16[3584,512]{1,0:T(8,128)(2,1)S(1)} custom-call(bf16[3584,512]{1,0:T(8,128)(2,1)} %m_ref.1, f32[2,512,512]{2,1,0:T(8,128)} %u_hbm.1, f32[2,512,512]{2,1,0:T(8,128)} %l_hbm.1), custom_call_target="tpu_custom_call" | custom-call | tf_op jit(solution)/shard_map/pallas_call | solution.py:340
  101.2 1.8 %copy.5 = bf16[3584,512]{1,0:T(8,128)(2,1)} copy(bf16[3584,512]{1,0:T(8,128)(2,1)S(1)} %shard_map.37) | data formatting | bytes 7340032
